TPU v7x, 128 devices: a whole 4x4x4 slice. The times are simulated.
128 devices in a mesh: expert: 4 (over z), seq: 4 (over y), tensor: 8 (over x, core).
Axes of the slice: x: 4, y: 4, z: 4, core: 2. Of those that a mesh axis runs over, the one named last changes fastest.
Arguments:
- tokens: bfloat16 [3072, 7168], P(('expert', 'seq')), may hold values from -6 to 6
- grad_out: bfloat16 [3072, 7168], P(('expert', 'seq')), may hold values from -6 to 6
- expert_ids: int32 [3072, 2], P(('expert', 'seq')), may hold values from 0 to 3, all different within a row; in each aligned block of 192 rows (0 to 191, 192 to 383, ...) at most 128 rows name the same one
- route_weights: bfloat16 [3072, 2], P(('expert', 'seq')), may hold values from 0.099609375 to 1
- gate_weight: bfloat16 [4, 7168, 2048], P('expert', 'seq', 'tensor'), may hold values from -0.0625 to 0.0625
- up_weight: bfloat16 [4, 7168, 2048], P('expert', 'seq', 'tensor'), may hold values from -0.0625 to 0.0625
- down_weight: bfloat16 [4, 7168, 2048], P('expert', 'seq', 'tensor'), may hold values from -0.125 to 0.125
Outputs:
- grad_tokens: bfloat16 [3072, 7168], P(('expert', 'seq'), 'tensor')
- grad_route: float32 [3072, 2], P(('expert', 'seq'))
- grad_gate: float32 [4, 7168, 2048], P('expert', 'seq', 'tensor')
- grad_up: float32 [4, 7168, 2048], P('expert', 'seq', 'tensor')
- grad_down: float32 [4, 7168, 2048], P('expert', 'seq', 'tensor')
Inputs may be any that keep to these rules, and one draw needn't show every extreme that they name: `expert_ids`: the two ids of a row differ. Within each aligned block of 192 rows (the tokens of one group of the expert and seq axes) no expert is named by more than 128 rows, and in some block an expert is named by exactly 128 rows.
All inputs are finite; a program needn't handle non-finite values.
Results may differ from a plain program's by a relative error of at most 0.019.
Values may be sent and summed in bfloat16 or wider, within the bound.
A program may use at most 192 MiB of HBM per device.

v0:
```python
import jax
import jax.numpy as jnp
from jax import lax
from jax.sharding import PartitionSpec as P


def shards(tokens, grad_out, expert_ids, route_weights, gate_weight, up_weight, down_weight):
    expert_count = lax.axis_size("expert")
    seq_count = lax.axis_size("seq")
    tensor_count = lax.axis_size("tensor")
    local_count = gate_weight.shape[0]
    tok_rows = tokens.shape[0]
    model_width = tokens.shape[1]
    part_width = model_width // tensor_count
    per_peer = tok_rows // 6
    peer_count = expert_count * seq_count
    block_rows = local_count * per_peer
    slot_count = peer_count * block_rows
    flat_ids = expert_ids.reshape(-1)
    route_count = flat_ids.shape[0]
    onehot = (
        flat_ids[:, None] == jnp.arange(local_count * expert_count, dtype=jnp.int32)[None, :]
    ).astype(jnp.int32)
    before = jnp.cumsum(onehot, axis=0) - onehot
    ranking = jnp.sum(before * onehot, axis=1)
    local_expert = flat_ids % local_count
    dest_peer = flat_ids // local_count * seq_count + ranking % seq_count
    target = (dest_peer * local_count + local_expert) * per_peer + ranking // seq_count
    source = (
        jnp.full((slot_count,), -1, jnp.int32)
        .at[target]
        .set(jnp.arange(route_count, dtype=jnp.int32))
    )
    filled = source >= 0
    safe_source = jnp.maximum(source, 0)
    token_of = safe_source // 2
    keep = filled[:, None].astype(tokens.dtype)
    weight_send = (
        route_weights.reshape(-1)[safe_source] * filled.astype(route_weights.dtype)
    ).reshape(peer_count, block_rows)
    in_send = (tokens[token_of] * keep).reshape(peer_count, block_rows, model_width)
    out_send = (grad_out[token_of] * keep).reshape(peer_count, block_rows, model_width)
    in_recv, out_recv, weight_recv = (
        lax.all_to_all(in_send, ("expert", "seq"), split_axis=0, concat_axis=0, tiled=True),
        lax.all_to_all(out_send, ("expert", "seq"), split_axis=0, concat_axis=0, tiled=True),
        lax.all_to_all(weight_send, ("expert", "seq"), split_axis=0, concat_axis=0, tiled=True),
    )

    def by_expert(values):
        shaped = values.reshape((peer_count, local_count, per_peer) + values.shape[2:])
        return jnp.swapaxes(shaped, 0, 1).reshape(
            (local_count, peer_count * per_peer) + values.shape[2:]
        )

    def by_peer(values):
        shaped = values.reshape((local_count, peer_count, per_peer) + values.shape[2:])
        return jnp.swapaxes(shaped, 0, 1).reshape((peer_count, block_rows) + values.shape[2:])

    in_rows = by_expert(in_recv)
    out_rows = by_expert(out_recv)
    prob = by_expert(weight_recv).astype(jnp.float32)[:, :, None]
    gate_full, up_full, down_full = (
        lax.all_gather(gate_weight, "seq", axis=1, tiled=True),
        lax.all_gather(up_weight, "seq", axis=1, tiled=True),
        lax.all_gather(down_weight, "seq", axis=1, tiled=True),
    )
    pre_gate = jnp.einsum("emd,edf->emf", in_rows, gate_full, preferred_element_type=jnp.float32)
    pre_up = jnp.einsum("emd,edf->emf", in_rows, up_full, preferred_element_type=jnp.float32)
    sigmoid_gate = jax.nn.sigmoid(pre_gate)
    silu_gate = pre_gate * sigmoid_gate
    hidden = silu_gate * pre_up
    hidden_low = hidden.astype(jnp.bfloat16)
    back_proj = jnp.einsum("emd,edf->emf", out_rows, down_full, preferred_element_type=jnp.float32)
    partial_scores = jnp.sum(hidden * back_proj, axis=2)
    scaled = (prob * out_rows.astype(jnp.float32)).astype(jnp.bfloat16)
    hidden_grad = prob * back_proj
    up_grad = (hidden_grad * silu_gate).astype(jnp.bfloat16)
    gate_grad = (
        hidden_grad * pre_up * sigmoid_gate * (1.0 + pre_gate * (1.0 - sigmoid_gate))
    ).astype(jnp.bfloat16)
    input_terms = jnp.einsum(
        "emf,edf->emd", gate_grad, gate_full, preferred_element_type=jnp.float32
    )
    input_terms = input_terms + jnp.einsum(
        "emf,edf->emd", up_grad, up_full, preferred_element_type=jnp.float32
    )
    route_scores = lax.psum(partial_scores, "tensor")
    input_shards = lax.psum_scatter(
        input_terms.astype(jnp.bfloat16), "tensor", scatter_dimension=2, tiled=True
    ).astype(jnp.float32)
    back_rows, back_scores = (
        lax.all_to_all(
            by_peer(input_shards).astype(jnp.bfloat16),
            ("expert", "seq"),
            split_axis=0,
            concat_axis=0,
            tiled=True,
        ).astype(jnp.float32),
        lax.all_to_all(
            by_peer(route_scores).astype(jnp.bfloat16),
            ("expert", "seq"),
            split_axis=0,
            concat_axis=0,
            tiled=True,
        ).astype(jnp.float32),
    )
    route_rows = back_rows.reshape(slot_count, part_width)[target].reshape(tok_rows, 2, part_width)
    grad_tokens = jnp.sum(route_rows, axis=1).astype(jnp.bfloat16)
    grad_route = back_scores.reshape(slot_count)[target].reshape(tok_rows, 2)
    gate_part = jnp.einsum("emd,emf->edf", in_rows, gate_grad, preferred_element_type=jnp.float32)
    up_part = jnp.einsum("emd,emf->edf", in_rows, up_grad, preferred_element_type=jnp.float32)
    down_part = jnp.einsum("emd,emf->edf", scaled, hidden_low, preferred_element_type=jnp.float32)
    grad_gate, grad_up, grad_down = (
        lax.psum_scatter(
            gate_part.astype(jnp.bfloat16), "seq", scatter_dimension=1, tiled=True
        ).astype(jnp.float32),
        lax.psum_scatter(
            up_part.astype(jnp.bfloat16), "seq", scatter_dimension=1, tiled=True
        ).astype(jnp.float32),
        lax.psum_scatter(
            down_part.astype(jnp.bfloat16), "seq", scatter_dimension=1, tiled=True
        ).astype(jnp.float32),
    )
    return (grad_tokens, grad_route, grad_gate, grad_up, grad_down)


def solution(mesh):
    placed = (
        P(("expert", "seq"), None),
        P(("expert", "seq"), None),
        P(("expert", "seq"), None),
        P(("expert", "seq"), None),
        P("expert", "seq", "tensor"),
        P("expert", "seq", "tensor"),
        P("expert", "seq", "tensor"),
    )
    return jax.shard_map(
        shards,
        mesh=mesh,
        in_specs=placed,
        out_specs=(
            P(("expert", "seq"), "tensor"),
            P(("expert", "seq"), None),
            P("expert", "seq", "tensor"),
            P("expert", "seq", "tensor"),
            P("expert", "seq", "tensor"),
        ),
        check_vma=False,
    )
```

profile of v0, /device:TPU:1, one launch (start us, length us, event | category | flops | bytes accessed | tf_op | source)
XLA Modules:
  0.0 604.9 jit_solution(13995530741329707157)
XLA Ops:
  7.2 0.7 all-gather.6.cloned.1.call-update
  7.9 0.9 copy.24
  8.8 0.1 eq.32
  8.9 0.1 eq.28
  9.1 0.7 broadcast_multiply_fusion.2
  9.8 1.2 reduce-window.6
  11.0 0.2 slice_reduce_fusion
  11.2 0.2 reduce-window.9
  11.4 0.1 add_bitcast_fusion
  11.5 0.1 copy.23
  11.6 0.1 mul.115
  11.8 2.9 scatter_custom_fusion
  14.7 0.8 copy.26
  15.6 0.2 reshape.290
  15.7 3.5 gather_fusion
  19.3 0.7 all_to_all.25
  20.0 8.6 %all-to-all-start = ((bf16[16,1,32]{2,1,0:T(2,128)(2,1)}), bf16[16,1,32]{2,1,0:T(2,128)(2,1)S(1)}, u32[]{:S(2)}, u32[]{:S(2)}) async-start(bf16[16,1,32]{2,1,0:T(2,128)(2,1)} %all_to_all.25), calls=%async_computation | async-start | bytes 16384 | tf_op jit(solution)/shard_map/all_to_all | solution.py:46
  28.6 0.1 reshape.301
  28.7 7.1 %gather_fusion.1 = bf16[512,7168]{1,0:T(8,128)(2,1)} fusion(bf16[192,7168]{1,0:T(8,128)(2,1)S(1)} %copy-done, s32[1024]{0:T(1024)S(1)} %get-tuple-element.29), kind=kCustom, calls=%fused_computation.1 | custom fusion | bytes 14682112 | tf_op jit(solution)/shard_map/gather | solution.py:42
  35.7 15.9 %gather_fusion.2 = bf16[512,7168]{1,0:T(8,128)(2,1)} fusion(bf16[192,7168]{1,0:T(8,128)(2,1)} %param.7, s32[1024]{0:T(1024)S(1)} %get-tuple-element.29), kind=kCustom, calls=%fused_computation.2 | custom fusion | bytes 14682112 | tf_op jit(solution)/shard_map/gather | solution.py:41
  51.6 10.6 %broadcast_multiply_fusion.1 = (bf16[16,32,7168]{2,1,0:T(8,128)(2,1)}, bf16[16,32,7168]{2,1,0:T(8,128)(2,1)}) fusion(bf16[16,32,7168]{2,1,0:T(8,128)(2,1)} %bitcast.67, bf16[16,32]{1,0:T(8,128)(2,1)S(1)} %reshape.301, bf16[16,32,7168]{2,1,0:T(8,128)(2,1)} %bitcast.68), kind=kLoop, calls=%fused_computation.27 | loop fusion | flops 7340032 | bytes 29361152 | tf_op jit(solution)/shard_map/mul | solution.py:42
  62.2 6.7 %all-to-all-start.2 = ((bf16[16,32,7168]{2,1,0:T(8,128)(2,1)}), bf16[16,32,7168]{2,1,0:T(8,128)(2,1)}, u32[]{:S(2)}, u32[]{:S(2)}) async-start(bf16[16,32,7168]{2,1,0:T(8,128)(2,1)} %get-tuple-element.26), calls=%async_computation.2 | async-start | bytes 14680064 | tf_op jit(solution)/shard_map/all_to_all | solution.py:44
  68.9 0.0 all-gather.8.cloned.1.call-start
  69.0 0.7 all-gather.8.cloned.1.call-update
  69.7 124.9 %all-to-all-done.2 = bf16[16,32,7168]{2,1,0:T(8,128)(2,1)} async-done(((bf16[16,32,7168]{2,1,0:T(8,128)(2,1)}), bf16[16,32,7168]{2,1,0:T(8,128)(2,1)}, u32[]{:S(2)}, u32[]{:S(2)}) %all-to-all-start.2) | async-done | bytes 7340064 | tf_op jit(solution)/shard_map/all_to_all | solution.py:44
  194.6 4.7 all-to-all-start.1
  199.3 0.0 all-gather.4.cloned.1.call-start
  199.3 0.7 all-gather.4.cloned.1.call-update
  200.1 0.1 reshape.300
  200.2 6.2 %fusion.10 = f32[512,256]{0,1:T(8,128)S(1)} fusion(bf16[512,7168]{1,0:T(8,128)(2,1)} %bitcast.5, bf16[1,7168,256]{2,1,0:T(8,128)(2,1)} %all-gather.6.cloned.1.call-done), kind=kOutput, calls=%fused_computation.22 | convolution fusion | flops 1879048192 | bytes 11534336 | tf_op jit(solution)/shard_map/emd,edf->emf/dot_general | solution.py:68
  206.4 6.2 %fusion.7 = f32[512,256]{0,1:T(8,128)S(1)} fusion(bf16[512,7168]{1,0:T(8,128)(2,1)} %bitcast.5, bf16[1,7168,256]{2,1,0:T(8,128)(2,1)} %all-gather.8.cloned.1.call-done), kind=kOutput, calls=%fused_computation.19 | convolution fusion | flops 1879048192 | bytes 11534336 | tf_op jit(solution)/shard_map/emd,edf->emf/dot_general | solution.py:67
  212.7 80.3 %all-gather.4.cloned.1.call-done = bf16[1,7168,256]{2,1,0:T(8,128)(2,1)} async-done(((bf16[1,1792,256]{2,1,0:T(8,128)(2,1)}), bf16[1,7168,256]{2,1,0:T(8,128)(2,1)}) %all-gather.4.cloned.1.call-update) | async-done | bytes 3670032 | tf_op jit(solution)/shard_map/all_gather | solution.py:65
  293.0 30.6 %all-to-all-done.1 = bf16[16,32,7168]{2,1,0:T(8,128)(2,1)} async-done(((bf16[16,32,7168]{2,1,0:T(8,128)(2,1)}), bf16[16,32,7168]{2,1,0:T(8,128)(2,1)}, u32[]{:S(2)}, u32[]{:S(2)}) %all-to-all-start.1) | async-done | bytes 7340064 | tf_op jit(solution)/shard_map/all_to_all | solution.py:45
  323.6 6.6 %multiply_reduce_fusion = (f32[512]{0:T(512)S(1)}, bf16[512,256]{0,1:T(8,128)(2,1)S(1)}, bf16[512,256]{0,1:T(8,128)(2,1)S(1)}) fusion(f32[512,256]{0,1:T(8,128)S(1)} %fusion.10, f32[512,256]{0,1:T(8,128)S(1)} %fusion.7, f32[512]{0:T(512)S(1)} %reshape.300, bf16[512,7168]{1,0:T(8,128)(2,1)} %bitcast.2, bf16[1,7168,256]{2,1,0:T(8,128)(2,1)} %all-gather.4.cloned.1.call-done), kind=kOutput, calls=%fused_computation.30 | convolution fusion | flops 1881275904 | bytes 12587008 | tf_op jit(solution)/shard_map/emd,edf->emf/dot_general | solution.py:73
  330.2 7.3 %fusion.5 = f32[512,7168]{1,0:T(8,128)} fusion(bf16[512,256]{0,1:T(8,128)(2,1)S(1)} %get-tuple-element.23, bf16[1,7168,256]{2,1,0:T(8,128)(2,1)S(1)} %copy-done.3), kind=kOutput, calls=%fused_computation.17 | convolution fusion | flops 1879048192 | bytes 18612224 | tf_op jit(solution)/shard_map/emf,edf->emd/dot_general | solution.py:81
  337.5 10.4 %fusion = bf16[1,512,7168]{2,1,0:T(8,128)(2,1)} fusion(f32[512,7168]{1,0:T(8,128)} %fusion.5, bf16[512,256]{0,1:T(8,128)(2,1)S(1)} %get-tuple-element.24, bf16[1,7168,256]{2,1,0:T(8,128)(2,1)S(1)} %copy-done.2), kind=kOutput, calls=%fused_computation.8 | convolution fusion | flops 1886388224 | bytes 25952256 | tf_op jit(solution)/shard_map/emf,edf->emd/dot_general | solution.py:84
  347.9 31.6 %copy.30 = bf16[1,512,7168]{1,0,2:T(2,128)(2,1)} copy(bf16[1,512,7168]{2,1,0:T(8,128)(2,1)} %fusion) | data formatting | bytes 14680064
  379.5 10.3 %copy.36 = bf16[7168,1,512]{2,0,1:T(8,128)(2,1)} copy(bf16[7168,1,512]{2,1,0:T(2,128)(2,1)} %bitcast.66) | data formatting | bytes 14680064
  389.9 0.0 reduce-scatter.11.cloned.1.call-start
  390.0 8.0 %fusion.3 = bf16[1,7168,256]{2,1,0:T(8,128)(2,1)} fusion(bf16[512,7168]{1,0:T(8,128)(2,1)} %bitcast.2, f32[512]{0:T(512)S(1)} %reshape.300, f32[512,256]{0,1:T(8,128)S(1)} %fusion.10, f32[512,256]{0,1:T(8,128)S(1)} %fusion.7), kind=kOutput, calls=%fused_computation.14 | convolution fusion | flops 1892679680 | bytes 12060672 | tf_op jit(solution)/shard_map/emd,emf->edf/dot_general | solution.py:112
  397.9 0.0 reduce-scatter.7.cloned.1.call-start
  398.0 7.7 %fusion.1 = bf16[1,7168,256]{2,1,0:T(8,128)(2,1)} fusion(bf16[512,7168]{1,0:T(8,128)(2,1)} %bitcast.5, bf16[512,256]{0,1:T(8,128)(2,1)S(1)} %get-tuple-element.23), kind=kOutput, calls=%fused_computation.12 | convolution fusion | flops 1880883200 | bytes 11272192 | tf_op jit(solution)/shard_map/emd,emf->edf/dot_general | solution.py:110
  405.7 7.1 %fusion.2 = bf16[1,7168,256]{2,1,0:T(8,128)(2,1)} fusion(bf16[512,7168]{1,0:T(8,128)(2,1)} %bitcast.5, bf16[512,256]{0,1:T(8,128)(2,1)S(1)} %get-tuple-element.24), kind=kOutput, calls=%fused_computation.13 | convolution fusion | flops 1880883200 | bytes 11272192 | tf_op jit(solution)/shard_map/emd,emf->edf/dot_general | solution.py:111
  412.9 23.6 %psum.7 = bf16[1,512]{1,0:T(2,128)(2,1)S(1)} all-reduce(f32[1,512]{1,0:T(1,128)S(1)} %bitcast.71), channel_id=1, replica_groups=mesh['expert'=4,'seq'=4,'tensor'=8] {'tensor'}, use_global_device_ids=true, to_apply=%region_7.8 | all-reduce | flops 512 | bytes 3072 | tf_op jit(solution)/shard_map/psum | solution.py:87
  436.6 0.7 convert_element_type.144
  437.2 3.5 all-to-all-start.4
  440.8 2.1 reshape_bitcast_fusion
  442.9 3.3 copy.31
  446.2 0.8 all-to-all-done.4
  447.0 6.1 %all-to-all-start.3 = ((bf16[16,32,896]{2,1,0:T(8,128)(2,1)}), bf16[16,32,896]{2,1,0:T(8,128)(2,1)}, u32[]{:S(2)}, u32[]{:S(2)}) async-start(bf16[16,32,896]{2,1,0:T(8,128)(2,1)} %bitcast.9), calls=%async_computation.3 | async-start | bytes 1835008 | tf_op jit(solution)/shard_map/all_to_all | solution.py:92
  453.1 0.1 reshape.304
  453.2 2.8 gather_fusion.4
  456.0 0.1 reshape.299
  456.1 0.7 copy.29
  456.8 35.1 %reduce-scatter.11.cloned.1.call-done = bf16[1,1792,256]{2,1,0:T(8,128)(2,1)} async-done(((bf16[1,7168,256]{2,1,0:T(8,128)(2,1)}), bf16[1,1792,256]{2,1,0:T(8,128)(2,1)}) %reduce-scatter.11.cloned.1.call-update) | async-done | bytes 917520 | tf_op jit(solution)/shard_map/reduce_scatter | solution.py:120
  491.9 2.5 convert_element_type.141
  494.4 42.0 %reduce-scatter.7.cloned.1.call-done = bf16[1,1792,256]{2,1,0:T(8,128)(2,1)} async-done(((bf16[1,7168,256]{2,1,0:T(8,128)(2,1)}), bf16[1,1792,256]{2,1,0:T(8,128)(2,1)}) %reduce-scatter.7.cloned.1.call-update) | async-done | bytes 917520 | tf_op jit(solution)/shard_map/reduce_scatter | solution.py:114
  536.4 2.5 convert_element_type.132
  539.0 42.1 %reduce-scatter.9.cloned.1.call-done = bf16[1,1792,256]{2,1,0:T(8,128)(2,1)} async-done(((bf16[1,7168,256]{2,1,0:T(8,128)(2,1)}), bf16[1,1792,256]{2,1,0:T(8,128)(2,1)}) %reduce-scatter.9.cloned.1.call-update) | async-done | bytes 917520 | tf_op jit(solution)/shard_map/reduce_scatter | solution.py:117
  581.1 2.5 convert_element_type.135
  583.7 2.7 bitcast_convert_fusion
  586.4 4.7 gather_fusion.3
  591.1 3.0 reshape.298
  594.0 3.7 reduce_sum.33
  (32 shorter events, 0.4 us)
Async XLA Ops:
  7.2 21.5 %copy-start = (bf16[192,7168]{1,0:T(8,128)(2,1)S(1)}, bf16[192,7168]{1,0:T(8,128)(2,1)}, u32[]{:S(2)}) copy-start(bf16[192,7168]{1,0:T(8,128)(2,1)} %param.8) | copy-start | bytes 8257540
  7.2 193.0 %all-gather.6.cloned.1.call-start = ((), (), s32[]{:S(2)}) async-start(), calls=%async_computation.10 | async-start | bytes 4587520 | tf_op jit(solution)/shard_map/all_gather | solution.py:64
  20.0 42.2 %all-to-all-start = ((bf16[16,1,32]{2,1,0:T(2,128)(2,1)}), bf16[16,1,32]{2,1,0:T(2,128)(2,1)S(1)}, u32[]{:S(2)}, u32[]{:S(2)}) async-start(bf16[16,1,32]{2,1,0:T(2,128)(2,1)} %all_to_all.25), calls=%async_computation | async-start | bytes 16384 | tf_op jit(solution)/shard_map/all_to_all | solution.py:46
  62.2 132.4 %all-to-all-start.2 = ((bf16[16,32,7168]{2,1,0:T(8,128)(2,1)}), bf16[16,32,7168]{2,1,0:T(8,128)(2,1)}, u32[]{:S(2)}, u32[]{:S(2)}) async-start(bf16[16,32,7168]{2,1,0:T(8,128)(2,1)} %get-tuple-element.26), calls=%async_computation.2 | async-start | bytes 14680064 | tf_op jit(solution)/shard_map/all_to_all | solution.py:44
  68.9 137.5 %all-gather.8.cloned.1.call-start = ((), (), s32[]{:S(2)}) async-start(), calls=%async_computation.11 | async-start | bytes 4587520 | tf_op jit(solution)/shard_map/all_gather | solution.py:63
  194.6 129.0 %all-to-all-start.1 = ((bf16[16,32,7168]{2,1,0:T(8,128)(2,1)}), bf16[16,32,7168]{2,1,0:T(8,128)(2,1)}, u32[]{:S(2)}, u32[]{:S(2)}) async-start(bf16[16,32,7168]{2,1,0:T(8,128)(2,1)} %get-tuple-element.25), calls=%async_computation.1 | async-start | bytes 14680064 | tf_op jit(solution)/shard_map/all_to_all | solution.py:45
  199.3 93.7 %all-gather.4.cloned.1.call-start = ((), (), s32[]{:S(2)}) async-start(), calls=%async_computation.9 | async-start | bytes 4587520 | tf_op jit(solution)/shard_map/all_gather | solution.py:65
  200.0 240.7 %reduce-scatter.13.cloned.1.call-start = ((), (), s32[]{:S(2)}) async-start(), calls=%async_computation.15 | async-start | bytes 8257536
  323.6 6.6 %copy-start.3 = (bf16[1,7168,256]{2,1,0:T(8,128)(2,1)S(1)}, bf16[1,7168,256]{2,1,0:T(8,128)(2,1)}, u32[]{:S(2)}) copy-start(bf16[1,7168,256]{2,1,0:T(8,128)(2,1)} %all-gather.8.cloned.1.call-done) | copy-start | bytes 11010052
  330.2 7.4 %copy-start.2 = (bf16[1,7168,256]{2,1,0:T(8,128)(2,1)S(1)}, bf16[1,7168,256]{2,1,0:T(8,128)(2,1)}, u32[]{:S(2)}) copy-start(bf16[1,7168,256]{2,1,0:T(8,128)(2,1)} %all-gather.6.cloned.1.call-done) | copy-start | bytes 11010052
  389.9 102.0 %reduce-scatter.11.cloned.1.call-start = ((), (), s32[]{:S(2)}) async-start(), calls=%async_computation.14 | async-start | bytes 4587520 | tf_op jit(solution)/shard_map/reduce_scatter | solution.py:120
  397.9 138.5 %reduce-scatter.7.cloned.1.call-start = ((), (), s32[]{:S(2)}) async-start(), calls=%async_computation.12 | async-start | bytes 4587520 | tf_op jit(solution)/shard_map/reduce_scatter | solution.py:114
  405.7 175.4 %reduce-scatter.9.cloned.1.call-start = ((), (), s32[]{:S(2)}) async-start(), calls=%async_computation.13 | async-start | bytes 4587520 | tf_op jit(solution)/shard_map/reduce_scatter | solution.py:117
  437.2 9.7 %all-to-all-start.4 = ((bf16[16,1,32]{2,1,0:T(2,128)(2,1)}), bf16[16,1,32]{2,1,0:T(2,128)(2,1)S(1)}, u32[]{:S(2)}, u32[]{:S(2)}) async-start(bf16[16,1,32]{2,1,0:T(2,128)(2,1)} %convert_element_type.144), calls=%async_computation.4 | async-start | bytes 16384 | tf_op jit(solution)/shard_map/all_to_all | solution.py:99
  447.0 136.7 %all-to-all-start.3 = ((bf16[16,32,896]{2,1,0:T(8,128)(2,1)}), bf16[16,32,896]{2,1,0:T(8,128)(2,1)}, u32[]{:S(2)}, u32[]{:S(2)}) async-start(bf16[16,32,896]{2,1,0:T(8,128)(2,1)} %bitcast.9), calls=%async_computation.3 | async-start | bytes 1835008 | tf_op jit(solution)/shard_map/all_to_all | solution.py:92
  583.7 14.1 %copy-start.1 = (bf16[192,7168]{1,0:T(8,128)(2,1)S(1)}, bf16[192,7168]{1,0:T(8,128)(2,1)}, u32[]{:S(2)}) copy-start(bf16[192,7168]{1,0:T(8,128)(2,1)} %param.8) | copy-start | bytes 8257540
Sparse Core Ops, SparseCore 0:
  9.7 47.2 all-gather.5
  71.4 91.2 all-gather.7
  201.8 91.1 all-gather.3
  390.0 46.9 reduce-scatter.12
  439.2 52.5 reduce-scatter.10
  494.1 42.2 reduce-scatter.6
  538.8 42.2 reduce-scatter.8
where the time goes:
time: 615 us; the launch traced here: 605 us
  waiting for transfers between devices  358 us (58%)
  local copies, waits for them, and re-layouts  92.3 us (15%)
  matrix products  59.6 us (10%)
  starting transfers between devices  29.8 us (5%)
  other arithmetic  26.9 us (4%)
  blocking collectives  23.6 us (4%)
  between operations  14.6 us (2%)
    all_to_all x1, waiting for transfers between devices, shards(): lax.all_to_all(in_send, ('expert', 'seq'), split_axis=0, concat_axis=0, t...  125 us
    all_gather x1, waiting for transfers between devices, shards(): lax.all_gather(down_weight, 'seq', axis=1, tiled=True)  80.3 us
    unnamed x15, local copies, waits for them, and re-layouts  49.8 us
    reduce_scatter x1, waiting for transfers between devices, shards(): lax.psum_scatter(up_part.astype(jnp.bfloat16), 'seq', scatter_dimension=1...  42.1 us
    reduce_scatter x1, waiting for transfers between devices, shards(): lax.psum_scatter(gate_part.astype(jnp.bfloat16), 'seq', scatter_dimension...  42 us
    reduce_scatter x1, waiting for transfers between devices, shards(): lax.psum_scatter(down_part.astype(jnp.bfloat16), 'seq', scatter_dimension...  35.1 us
    all_to_all x1, waiting for transfers between devices, shards(): lax.all_to_all(out_send, ('expert', 'seq'), split_axis=0, concat_axis=0,...  30.6 us
    psum x1, blocking collectives, shards(): route_scores = lax.psum(partial_scores, 'tensor')  23.6 us
  transfers between devices with their start and end apart: 12, of which 7 were waited for; matrix products, arithmetic and copies ran while one was open for 16% of the time, Pallas kernels for 0%

commit v1 on v0

--- a/solution.py
+++ b/solution.py
@@ -5,6 +5,27 @@
 
 
 def shards(tokens, grad_out, expert_ids, route_weights, gate_weight, up_weight, down_weight):
+
+    def entries_watch(own_rows):
+        size_here = lax.axis_size("seq")
+        runs = []
+        for dev_i in range(size_here):
+            runs.append((dev_i, (dev_i + 1) % size_here))
+        log = []
+        for dev_i in range(size_here):
+            log.append((dev_i, (dev_i - 1) % size_here))
+        heard, ready = ([own_rows], [own_rows])
+        for _ in range(size_here // 2):
+            mat_out = lax.ppermute(heard[-1], "seq", runs)
+            heard.append(mat_out)
+        for _ in range((size_here - 1) // 2):
+            ready.append(lax.ppermute(ready[-1], "seq", log))
+        return jnp.roll(
+            jnp.concatenate([*heard[::-1], *ready[1:]], axis=1),
+            shift=(lax.axis_index("seq") - size_here // 2) * own_rows.shape[1],
+            axis=1,
+        )
+
     expert_count = lax.axis_size("expert")
     seq_count = lax.axis_size("seq")
     tensor_count = lax.axis_size("tensor")
@@ -62,7 +83,7 @@
     gate_full, up_full, down_full = (
         lax.all_gather(gate_weight, "seq", axis=1, tiled=True),
         lax.all_gather(up_weight, "seq", axis=1, tiled=True),
-        lax.all_gather(down_weight, "seq", axis=1, tiled=True),
+        entries_watch(down_weight),
     )
     pre_gate = jnp.einsum("emd,edf->emf", in_rows, gate_full, preferred_element_type=jnp.float32)
     pre_up = jnp.einsum("emd,edf->emf", in_rows, up_full, preferred_element_type=jnp.float32)

time: 615 us -> 677 us (1.10)
  waiting for transfers between devices: 358 us -> 394 us
  starting transfers between devices: 29.8 us -> 44 us
  local copies, waits for them, and re-layouts: 92.3 us -> 103 us
    ppermute x0 -> x3, waiting for transfers between devices: none -> 147 us  [the longest x2 147 us: entries_watch(): mat_out = lax.ppermute(heard[-1], 'seq', runs)]
    all_gather x1 -> x0, waiting for transfers between devices: 80.3 us -> none  [shards(): lax.all_gather(down_weight, 'seq', axis=1, tiled=True)]
    all_to_all x1, waiting for transfers between devices: 30.6 us -> 0.01 us  [shards(): lax.all_to_all(out_send, ('expert', 'seq'), split_axis=0, concat_axis=0,...]
    ppermute x0 -> x3, starting transfers between devices: none -> 13 us  [the longest x1 7.51 us: entries_watch(): ready.append(lax.ppermute(ready[-1], 'seq', log))]
    unnamed x15 -> x24, local copies, waits for them, and re-layouts: 49.8 us -> 59.3 us
    reduce_scatter x1, waiting for transfers between devices: 35.1 us -> 42 us  [shards(): lax.psum_scatter(down_part.astype(jnp.bfloat16), 'seq', scatter_dimension...]
  transfers between devices with their start and end apart: 12 -> 14, of which waited for: 7 -> 7; matrix products, arithmetic and copies ran while one was open for 16% -> 14% of each run, Pallas kernels for 0% -> 0%
where the time goes in v1:
time: 677 us; the launch traced here: 667 us
  waiting for transfers between devices  394 us (58%)
  local copies, waits for them, and re-layouts  103 us (15%)
  matrix products  59 us (9%)
  starting transfers between devices  44 us (6%)
  other arithmetic  26.9 us (4%)
  blocking collectives  25.6 us (4%)
  between operations  14.8 us (2%)
    ppermute x2, waiting for transfers between devices, entries_watch(): mat_out = lax.ppermute(heard[-1], 'seq', runs)  147 us
    all_to_all x1, waiting for transfers between devices, shards(): lax.all_to_all(in_send, ('expert', 'seq'), split_axis=0, concat_axis=0, t...  125 us
    unnamed x24, local copies, waits for them, and re-layouts  59.3 us
    reduce_scatter x1, waiting for transfers between devices, shards(): lax.psum_scatter(down_part.astype(jnp.bfloat16), 'seq', scatter_dimension...  42 us
    reduce_scatter x1, waiting for transfers between devices, shards(): lax.psum_scatter(up_part.astype(jnp.bfloat16), 'seq', scatter_dimension=1...  42 us
    reduce_scatter x1, waiting for transfers between devices, shards(): lax.psum_scatter(gate_part.astype(jnp.bfloat16), 'seq', scatter_dimension...  35.7 us
    psum x1, blocking collectives, shards(): route_scores = lax.psum(partial_scores, 'tensor')  25.6 us
    gather x1, local copies, waits for them, and re-layouts, shards(): tokens[token_of] * keep  15.9 us
  transfers between devices with their start and end apart: 14, of which 7 were waited for; matrix products, arithmetic and copies ran while one was open for 14% of the time, Pallas kernels for 0%

profile of v1, /device:TPU:1, one launch (start us, length us, event | category | flops | bytes accessed | tf_op | source)
XLA Modules:
  0.0 666.7 jit_solution(17652051321747972400)
XLA Ops:
  7.2 0.9 copy.24
  8.1 0.1 eq.35
  8.3 0.1 eq.31
  8.4 0.7 broadcast_multiply_fusion.2
  9.1 1.2 reduce-window.6
  10.3 0.2 slice_reduce_fusion
  10.5 0.2 reduce-window.9
  10.9 0.1 mul.118
  11.1 2.9 scatter_custom_fusion
  14.1 0.8 copy.26
  14.9 0.2 reshape.290
  15.1 3.5 gather_fusion
  18.6 0.7 all_to_all.25
  19.3 8.6 %all-to-all-start = ((bf16[16,1,32]{2,1,0:T(2,128)(2,1)}), bf16[16,1,32]{2,1,0:T(2,128)(2,1)S(1)}, u32[]{:S(2)}, u32[]{:S(2)}) async-start(bf16[16,1,32]{2,1,0:T(2,128)(2,1)} %all_to_all.25), calls=%async_computation | async-start | bytes 16384 | tf_op jit(solution)/shard_map/all_to_all | solution.py:67
  28.0 7.1 %gather_fusion.1 = bf16[512,7168]{1,0:T(8,128)(2,1)} fusion(bf16[192,7168]{1,0:T(8,128)(2,1)S(1)} %copy-done, s32[1024]{0:T(1024)S(1)} %get-tuple-element.29), kind=kCustom, calls=%fused_computation.1 | custom fusion | bytes 14682112 | tf_op jit(solution)/shard_map/gather | solution.py:63
  35.1 15.9 %gather_fusion.2 = bf16[512,7168]{1,0:T(8,128)(2,1)} fusion(bf16[192,7168]{1,0:T(8,128)(2,1)} %param.7, s32[1024]{0:T(1024)S(1)} %get-tuple-element.29), kind=kCustom, calls=%fused_computation.2 | custom fusion | bytes 14682112 | tf_op jit(solution)/shard_map/gather | solution.py:62
  50.9 10.6 %broadcast_multiply_fusion.1 = (bf16[16,32,7168]{2,1,0:T(8,128)(2,1)}, bf16[16,32,7168]{2,1,0:T(8,128)(2,1)}) fusion(bf16[16,32,7168]{2,1,0:T(8,128)(2,1)} %bitcast.67, bf16[16,32]{1,0:T(8,128)(2,1)S(1)} %reshape.301, bf16[16,32,7168]{2,1,0:T(8,128)(2,1)} %bitcast.68), kind=kLoop, calls=%fused_computation.28 | loop fusion | flops 7340032 | bytes 29361152 | tf_op jit(solution)/shard_map/mul | solution.py:63
  61.5 6.7 %all-to-all-start.2 = ((bf16[16,32,7168]{2,1,0:T(8,128)(2,1)}), bf16[16,32,7168]{2,1,0:T(8,128)(2,1)}, u32[]{:S(2)}, u32[]{:S(2)}) async-start(bf16[16,32,7168]{2,1,0:T(8,128)(2,1)} %get-tuple-element.26), calls=%async_computation.2 | async-start | bytes 14680064 | tf_op jit(solution)/shard_map/all_to_all | solution.py:65
  68.3 0.7 all-gather.3.cloned.1.call-update
  69.0 124.9 %all-to-all-done.2 = bf16[16,32,7168]{2,1,0:T(8,128)(2,1)} async-done(((bf16[16,32,7168]{2,1,0:T(8,128)(2,1)}), bf16[16,32,7168]{2,1,0:T(8,128)(2,1)}, u32[]{:S(2)}, u32[]{:S(2)}) %all-to-all-start.2) | async-done | bytes 7340064 | tf_op jit(solution)/shard_map/all_to_all | solution.py:65
  193.9 4.8 all-to-all-start.1
  198.8 0.7 all-gather.5.cloned.1.call-update
  199.5 1.3 collective-permute-start
  200.8 129.2 %collective-permute-done = bf16[1,1792,256]{2,1,0:T(8,128)(2,1)S(1)} collective-permute-done((bf16[1,1792,256]{2,1,0:T(8,128)(2,1)S(1)}, bf16[1,1792,256]{2,1,0:T(8,128)(2,1)S(1)}, u32[]{:S(2)}, u32[]{:S(2)}) %collective-permute-start) | collective-permute-done | bytes 917536 | tf_op jit(solution)/shard_map/ppermute | solution.py:19
  330.0 4.2 collective-permute-start.1
  334.2 7.5 %collective-permute-start.2 = (bf16[1,1792,256]{2,1,0:T(8,128)(2,1)S(1)}, bf16[1,1792,256]{2,1,0:T(8,128)(2,1)S(1)}, u32[]{:S(2)}, u32[]{:S(2)}) collective-permute-start(bf16[1,1792,256]{2,1,0:T(8,128)(2,1)S(1)} %copy-done.3), channel_id=1, source_target_pairs={{0,24},{8,0},{16,8},{24,16},{1,25},{9,1},{17,9},{25,17},{2,26},{10... | collective-permute-start | bytes 2752520 | tf_op jit(solution)/shard_map/ppermute | solution.py:22
  341.8 17.4 %collective-permute-done.1 = bf16[1,1792,256]{2,1,0:T(8,128)(2,1)} collective-permute-done((bf16[1,1792,256]{2,1,0:T(8,128)(2,1)S(1)}, bf16[1,1792,256]{2,1,0:T(8,128)(2,1)}, u32[]{:S(2)}, u32[]{:S(2)}) %collective-permute-start.1) | collective-permute-done | bytes 917536 | tf_op jit(solution)/shard_map/ppermute | solution.py:19
  359.1 2.2 constant_dynamic-update-slice_fusion.7
  361.3 1.0 constant_dynamic-update-slice_fusion.6
  362.3 1.0 constant_dynamic-update-slice_fusion.5
  363.3 1.0 constant_dynamic-update-slice_fusion.4
  364.4 2.2 constant_dynamic-update-slice_fusion.3
  366.5 1.0 constant_dynamic-update-slice_fusion.2
  367.5 1.1 constant_dynamic-update-slice_fusion.1
  368.6 1.0 constant_dynamic-update-slice_fusion
  369.6 6.2 fusion.10
  375.8 6.2 fusion.7
  382.1 6.6 multiply_reduce_fusion
  388.7 7.4 %fusion.5 = f32[512,7168]{1,0:T(8,128)} fusion(bf16[512,256]{0,1:T(8,128)(2,1)S(1)} %get-tuple-element.23, bf16[1,7168,256]{2,1,0:T(8,128)(2,1)S(1)} %copy-done.4), kind=kOutput, calls=%fused_computation.17 | convolution fusion | flops 1879048192 | bytes 18612224 | tf_op jit(solution)/shard_map/emf,edf->emd/dot_general | solution.py:102
  396.1 10.4 %fusion = bf16[1,512,7168]{2,1,0:T(8,128)(2,1)} fusion(f32[512,7168]{1,0:T(8,128)} %fusion.5, bf16[512,256]{0,1:T(8,128)(2,1)S(1)} %get-tuple-element.24, bf16[1,7168,256]{2,1,0:T(8,128)(2,1)S(1)} %copy-done.2), kind=kOutput, calls=%fused_computation.8 | convolution fusion | flops 1886388224 | bytes 25952256 | tf_op jit(solution)/shard_map/emf,edf->emd/dot_general | solution.py:105
  406.5 31.6 %copy.30 = bf16[1,512,7168]{1,0,2:T(2,128)(2,1)} copy(bf16[1,512,7168]{2,1,0:T(8,128)(2,1)} %fusion) | data formatting | bytes 14680064
  438.1 10.3 %copy.36 = bf16[7168,1,512]{2,0,1:T(8,128)(2,1)} copy(bf16[7168,1,512]{2,1,0:T(2,128)(2,1)} %bitcast.66) | data formatting | bytes 14680064
  448.5 7.0 %fusion.1 = bf16[1,7168,256]{2,1,0:T(8,128)(2,1)} fusion(bf16[512,7168]{1,0:T(8,128)(2,1)} %bitcast.5, bf16[512,256]{0,1:T(8,128)(2,1)S(1)} %get-tuple-element.23), kind=kOutput, calls=%fused_computation.12 | convolution fusion | flops 1880883200 | bytes 11272192 | tf_op jit(solution)/shard_map/emd,emf->edf/dot_general | solution.py:131
  455.6 7.1 %fusion.2 = bf16[1,7168,256]{2,1,0:T(8,128)(2,1)} fusion(bf16[512,7168]{1,0:T(8,128)(2,1)} %bitcast.5, bf16[512,256]{0,1:T(8,128)(2,1)S(1)} %get-tuple-element.24), kind=kOutput, calls=%fused_computation.13 | convolution fusion | flops 1880883200 | bytes 11272192 | tf_op jit(solution)/shard_map/emd,emf->edf/dot_general | solution.py:132
  462.7 8.1 %fusion.3 = bf16[1,7168,256]{2,1,0:T(8,128)(2,1)} fusion(bf16[512,7168]{1,0:T(8,128)(2,1)} %bitcast.2, f32[512]{0:T(512)S(1)} %reshape.300, f32[512,256]{0,1:T(8,128)S(1)} %fusion.10, f32[512,256]{0,1:T(8,128)S(1)} %fusion.7), kind=kOutput, calls=%fused_computation.14 | convolution fusion | flops 1892679680 | bytes 12060672 | tf_op jit(solution)/shard_map/emd,emf->edf/dot_general | solution.py:133
  470.9 25.6 %psum.7 = bf16[1,512]{1,0:T(2,128)(2,1)S(1)} all-reduce(f32[1,512]{1,0:T(1,128)S(1)} %bitcast.71), channel_id=1, replica_groups=mesh['expert'=4,'seq'=4,'tensor'=8] {'tensor'}, use_global_device_ids=true, to_apply=%region_7.8 | all-reduce | flops 512 | bytes 3072 | tf_op jit(solution)/shard_map/psum | solution.py:108
  496.5 0.7 convert_element_type.144
  497.2 4.6 all-to-all-start.4
  501.8 2.1 reshape_bitcast_fusion
  503.9 3.3 copy.31
  507.2 0.8 all-to-all-done.4
  508.1 6.1 all-to-all-start.3
  514.3 2.8 gather_fusion.4
  517.3 0.7 copy.29
  517.9 35.7 %reduce-scatter.7.cloned.1.call-done = bf16[1,1792,256]{2,1,0:T(8,128)(2,1)} async-done(((bf16[1,7168,256]{2,1,0:T(8,128)(2,1)}), bf16[1,1792,256]{2,1,0:T(8,128)(2,1)}) %reduce-scatter.7.cloned.1.call-update) | async-done | bytes 917520 | tf_op jit(solution)/shard_map/reduce_scatter | solution.py:135
  553.7 2.5 convert_element_type.132
  556.2 42.0 %reduce-scatter.9.cloned.1.call-done = bf16[1,1792,256]{2,1,0:T(8,128)(2,1)} async-done(((bf16[1,7168,256]{2,1,0:T(8,128)(2,1)}), bf16[1,1792,256]{2,1,0:T(8,128)(2,1)}) %reduce-scatter.9.cloned.1.call-update) | async-done | bytes 917520 | tf_op jit(solution)/shard_map/reduce_scatter | solution.py:138
  598.2 2.5 convert_element_type.135
  600.8 42.0 %reduce-scatter.11.cloned.1.call-done = bf16[1,1792,256]{2,1,0:T(8,128)(2,1)} async-done(((bf16[1,7168,256]{2,1,0:T(8,128)(2,1)}), bf16[1,1792,256]{2,1,0:T(8,128)(2,1)}) %reduce-scatter.11.cloned.1.call-update) | async-done | bytes 917520 | tf_op jit(solution)/shard_map/reduce_scatter | solution.py:141
  642.8 2.5 convert_element_type.141
  645.3 2.7 bitcast_convert_fusion
  648.0 4.7 gather_fusion.3
  652.7 3.0 reshape.298
  655.7 3.7 reduce_sum.33
  (45 shorter events, 1.1 us)
Async XLA Ops:
  7.2 20.8 %copy-start = (bf16[192,7168]{1,0:T(8,128)(2,1)S(1)}, bf16[192,7168]{1,0:T(8,128)(2,1)}, u32[]{:S(2)}) copy-start(bf16[192,7168]{1,0:T(8,128)(2,1)} %param.8) | copy-start | bytes 8257540
  19.3 42.2 %all-to-all-start = ((bf16[16,1,32]{2,1,0:T(2,128)(2,1)}), bf16[16,1,32]{2,1,0:T(2,128)(2,1)S(1)}, u32[]{:S(2)}, u32[]{:S(2)}) async-start(bf16[16,1,32]{2,1,0:T(2,128)(2,1)} %all_to_all.25), calls=%async_computation | async-start | bytes 16384 | tf_op jit(solution)/shard_map/all_to_all | solution.py:67
  61.5 132.4 %all-to-all-start.2 = ((bf16[16,32,7168]{2,1,0:T(8,128)(2,1)}), bf16[16,32,7168]{2,1,0:T(8,128)(2,1)}, u32[]{:S(2)}, u32[]{:S(2)}) async-start(bf16[16,32,7168]{2,1,0:T(8,128)(2,1)} %get-tuple-element.26), calls=%async_computation.2 | async-start | bytes 14680064 | tf_op jit(solution)/shard_map/all_to_all | solution.py:65
  68.2 301.4 %all-gather.3.cloned.1.call-start = ((), (), s32[]{:S(2)}) async-start(), calls=%async_computation.9 | async-start | bytes 4587520 | tf_op jit(solution)/shard_map/all_gather | solution.py:85
  193.9 5.6 copy-start.3
  193.9 188.2 %all-to-all-start.1 = ((bf16[16,32,7168]{2,1,0:T(8,128)(2,1)}), bf16[16,32,7168]{2,1,0:T(8,128)(2,1)}, u32[]{:S(2)}, u32[]{:S(2)}) async-start(bf16[16,32,7168]{2,1,0:T(8,128)(2,1)} %get-tuple-element.25), calls=%async_computation.1 | async-start | bytes 14680064 | tf_op jit(solution)/shard_map/all_to_all | solution.py:66
  198.7 177.1 %all-gather.5.cloned.1.call-start = ((), (), s32[]{:S(2)}) async-start(), calls=%async_computation.10 | async-start | bytes 4587520 | tf_op jit(solution)/shard_map/all_gather | solution.py:84
  199.5 302.3 %reduce-scatter.13.cloned.1.call-start = ((), (), s32[]{:S(2)}) async-start(), calls=%async_computation.14 | async-start | bytes 8257536
  199.5 130.5 %collective-permute-start = (bf16[1,1792,256]{2,1,0:T(8,128)(2,1)S(1)}, bf16[1,1792,256]{2,1,0:T(8,128)(2,1)S(1)}, u32[]{:S(2)}, u32[]{:S(2)}) collective-permute-start(bf16[1,1792,256]{2,1,0:T(8,128)(2,1)S(1)} %copy-done.3), channel_id=1, source_target_pairs={{0,8},{8,16},{16,24},{24,0},{1,9},{9,17},{17,25},{25,1},{2,10},{10... | collective-permute-start | bytes 2752520 | tf_op jit(solution)/shard_map/ppermute | solution.py:19
  330.0 29.2 %collective-permute-start.1 = (bf16[1,1792,256]{2,1,0:T(8,128)(2,1)S(1)}, bf16[1,1792,256]{2,1,0:T(8,128)(2,1)}, u32[]{:S(2)}, u32[]{:S(2)}) collective-permute-start(bf16[1,1792,256]{2,1,0:T(8,128)(2,1)S(1)} %collective-permute-done), channel_id=1, source_target_pairs={{0,8},{8,16},{16,24},{24,0},{1,9},{9,17},{17,25},{25,1},{2,10},{10... | collective-permute-start | bytes 2752520 | tf_op jit(solution)/shard_map/ppermute | solution.py:19
  334.2 29.2 %collective-permute-start.2 = (bf16[1,1792,256]{2,1,0:T(8,128)(2,1)S(1)}, bf16[1,1792,256]{2,1,0:T(8,128)(2,1)S(1)}, u32[]{:S(2)}, u32[]{:S(2)}) collective-permute-start(bf16[1,1792,256]{2,1,0:T(8,128)(2,1)S(1)} %copy-done.3), channel_id=1, source_target_pairs={{0,24},{8,0},{16,8},{24,16},{1,25},{9,1},{17,9},{25,17},{2,26},{10... | collective-permute-start | bytes 2752520 | tf_op jit(solution)/shard_map/ppermute | solution.py:22
  382.1 6.6 copy-start.4
  388.7 7.4 %copy-start.2 = (bf16[1,7168,256]{2,1,0:T(8,128)(2,1)S(1)}, bf16[1,7168,256]{2,1,0:T(8,128)(2,1)}, u32[]{:S(2)}) copy-start(bf16[1,7168,256]{2,1,0:T(8,128)(2,1)} %all-gather.3.cloned.1.call-done) | copy-start | bytes 11010052
  448.5 105.2 %reduce-scatter.7.cloned.1.call-start = ((), (), s32[]{:S(2)}) async-start(), calls=%async_computation.11 | async-start | bytes 4587520 | tf_op jit(solution)/shard_map/reduce_scatter | solution.py:135
  455.6 142.7 %reduce-scatter.9.cloned.1.call-start = ((), (), s32[]{:S(2)}) async-start(), calls=%async_computation.12 | async-start | bytes 4587520 | tf_op jit(solution)/shard_map/reduce_scatter | solution.py:138
  462.7 180.1 %reduce-scatter.11.cloned.1.call-start = ((), (), s32[]{:S(2)}) async-start(), calls=%async_computation.13 | async-start | bytes 4587520 | tf_op jit(solution)/shard_map/reduce_scatter | solution.py:141
  497.2 10.9 %all-to-all-start.4 = ((bf16[16,1,32]{2,1,0:T(2,128)(2,1)}), bf16[16,1,32]{2,1,0:T(2,128)(2,1)S(1)}, u32[]{:S(2)}, u32[]{:S(2)}) async-start(bf16[16,1,32]{2,1,0:T(2,128)(2,1)} %convert_element_type.144), calls=%async_computation.4 | async-start | bytes 16384 | tf_op jit(solution)/shard_map/all_to_all | solution.py:120
  508.1 137.2 %all-to-all-start.3 = ((bf16[16,32,896]{2,1,0:T(8,128)(2,1)}), bf16[16,32,896]{2,1,0:T(8,128)(2,1)}, u32[]{:S(2)}, u32[]{:S(2)}) async-start(bf16[16,32,896]{2,1,0:T(8,128)(2,1)} %bitcast.9), calls=%async_computation.3 | async-start | bytes 1835008 | tf_op jit(solution)/shard_map/all_to_all | solution.py:113
  645.3 14.1 %copy-start.1 = (bf16[192,7168]{1,0:T(8,128)(2,1)S(1)}, bf16[192,7168]{1,0:T(8,128)(2,1)}, u32[]{:S(2)}) copy-start(bf16[192,7168]{1,0:T(8,128)(2,1)} %param.8) | copy-start | bytes 8257540
Sparse Core Ops, SparseCore 0:
  70.7 91.2 all-gather.2
  201.2 91.1 all-gather.4
  448.6 50.1 reduce-scatter.12
  501.1 52.5 reduce-scatter.6
  555.9 42.2 reduce-scatter.8
  600.5 42.2 reduce-scatter.10
